TPU v7x, 32 devices: a whole 2x2x4 slice. The times are simulated.
32 devices in a mesh: grp: 4 (over x, core), seq: 8 (over z, y).
Axes of the slice: x: 2, y: 2, z: 4, core: 2. Of those that a mesh axis runs over, the one named last changes fastest.
Arguments:
- signal: float32 [64, 2048, 768], P('grp', 'seq'), may hold values from -36 to 36
- entry_gain: float32 [768], replicated
- entry_shift: float32 [768], replicated, may hold values from -3 to 3
- dilated_kernel: float32 [3, 768, 384], replicated
- middle_gain: float32 [384], replicated
- middle_shift: float32 [384], replicated, may hold values from -3 to 3
- pointwise_kernel: float32 [384, 768], replicated
- pointwise_bias: float32 [768], replicated, may hold values from -3 to 3
- lengths: int32 [64], replicated, may hold values from 128 to 1024, as said below
- assignment: int32 [4, 16], P('grp'), may hold values from 0 to 15, as said below
- cotangent: float32 [65536, 768], P(('grp', 'seq')), may hold values from -6 to 6
Outputs:
- activations: float32 [65536, 768], P(('grp', 'seq'))
- signal_gradient: float32 [64, 2048, 768], P('grp', 'seq')
- entry_gain_gradient: float32 [768], replicated
- entry_shift_gradient: float32 [768], replicated
- dilated_kernel_gradient: float32 [3, 768, 384], replicated
- middle_gain_gradient: float32 [384], replicated
- middle_shift_gradient: float32 [384], replicated
- pointwise_kernel_gradient: float32 [384, 768], replicated
- pointwise_bias_gradient: float32 [768], replicated
Inputs may be any that keep to these rules, and one draw needn't show every extreme that they name: `lengths`: valid rows of a window come first; some window is full with 1024 rows and some has exactly 128. `assignment`: each row lists the 16 windows of one group once.
All inputs are finite; a program needn't handle non-finite values.
Results may differ from a plain program's by a relative error of at most 0.0066.
Values may be sent and summed in bfloat16 or wider, within the bound.
No kernel may reach another device: no remote copies, remote signals or barrier semaphores. Data moves between devices by JAX's collectives and lax.ppermute only.
A program may use at most 128 MiB of HBM per device.

v0:
```python
import jax
import jax.numpy as jnp
from jax import lax
from jax.sharding import PartitionSpec as P

DILATION_STEP = 38
WINDOW_SPAN = 1024
HALF_WINDOW_ROWS = 512
EPSILON = 0.001


def from_partner(block, axis, bit):
    count = lax.axis_size(axis)
    route = []
    for low in range(count):
        high = low | 1 << bit
        if high != low and high < count:
            route += [(low, high), (high, low)]
    return lax.ppermute(block, axis, route)


def smooth(values):
    return jax.nn.gelu(values, approximate=True)


def moments(values, valid_mask, row_count):
    centre = lax.psum(jnp.sum(values * valid_mask, axis=(0, 1)), ("grp", "seq")) / row_count
    deviation = (values - centre) * valid_mask
    spread = lax.psum(jnp.sum(deviation * deviation, axis=(0, 1)), ("grp", "seq")) / row_count
    return (centre, lax.rsqrt(spread + EPSILON))


def extended(resident_rows, neighbour_border):
    position_count = resident_rows.shape[0]
    channel_width = resident_rows.shape[2]
    empty_row_block = jnp.zeros((position_count, DILATION_STEP, channel_width), resident_rows.dtype)
    bottom_portion = jnp.concatenate(
        [empty_row_block, resident_rows[:, :HALF_WINDOW_ROWS], neighbour_border[:, DILATION_STEP:]],
        axis=1,
    )
    top_portion = jnp.concatenate(
        [neighbour_border[:, :DILATION_STEP], resident_rows[:, HALF_WINDOW_ROWS:], empty_row_block],
        axis=1,
    )
    return jnp.stack([bottom_portion, top_portion], axis=1).reshape(
        2 * position_count, HALF_WINDOW_ROWS + 2 * DILATION_STEP, channel_width
    )


def per_device(
    signal,
    entry_gain,
    entry_shift,
    dilated_kernel,
    middle_gain,
    middle_shift,
    pointwise_kernel,
    pointwise_bias,
    lengths,
    assignment,
    cotangent,
):
    seq_count = lax.axis_size("seq")
    seq_place = lax.axis_index("seq")
    grp_place = lax.axis_index("grp")
    group_windows, segment, channel_width = signal.shape
    source_rows = segment // 2
    position_count = group_windows // seq_count
    bin_pairs = signal.reshape(group_windows, source_rows, 2, channel_width)
    first_bin = bin_pairs[:, :, 0]
    second_bin = bin_pairs[:, :, 1]
    take_first = first_bin >= second_bin
    group_lengths = lax.dynamic_slice_in_dim(lengths, grp_place * group_windows, group_windows)
    source_position = seq_place * source_rows + jnp.arange(source_rows, dtype=jnp.int32)
    source_valid = (source_position[None, :] < group_lengths[:, None]).astype(jnp.float32)[
        :, :, None
    ]
    pooled_low = (jnp.where(take_first, first_bin, second_bin) * source_valid).astype(jnp.bfloat16)
    window_order = assignment[0]
    upper_source = (seq_place >= seq_count // 2).astype(jnp.int32)
    targets = jnp.arange(seq_count, dtype=jnp.int32)
    slot_range = jnp.arange(position_count, dtype=jnp.int32)
    picked = window_order[
        (
            jnp.bitwise_xor(targets, upper_source)[:, None] * position_count + slot_range[None, :]
        ).reshape(-1)
    ]
    outgoing = jnp.take(pooled_low, picked, axis=0)
    arrived = lax.all_to_all(outgoing, "seq", split_axis=0, concat_axis=1, tiled=True)
    partner_place = jnp.bitwise_xor(seq_place, 1)
    own_windows = lax.dynamic_slice_in_dim(window_order, seq_place * position_count, position_count)
    partner_windows = lax.dynamic_slice_in_dim(
        window_order, partner_place * position_count, position_count
    )
    row_position = jnp.arange(WINDOW_SPAN, dtype=jnp.int32)
    limit_rows = jnp.where(
        row_position[None, :] < HALF_WINDOW_ROWS,
        jnp.take(group_lengths, own_windows)[:, None],
        jnp.take(group_lengths, partner_windows)[:, None],
    )
    valid_mask = (row_position[None, :] < limit_rows).astype(jnp.float32)[:, :, None]
    row_count = jnp.sum(lengths.astype(jnp.float32))
    pooled = arrived.astype(jnp.float32)
    entry_centre, entry_scale = moments(pooled, valid_mask, row_count)
    entry_norm = (pooled - entry_centre) * entry_scale
    entry_smooth, entry_back = jax.vjp(smooth, entry_norm * entry_gain + entry_shift)
    entry_activation = (entry_smooth * valid_mask).astype(jnp.bfloat16)
    kernel_low = dilated_kernel.astype(jnp.bfloat16)
    entry_border = from_partner(
        entry_activation[:, HALF_WINDOW_ROWS - DILATION_STEP : HALF_WINDOW_ROWS + DILATION_STEP],
        "seq",
        0,
    )
    entry_widened = extended(entry_activation, entry_border)
    dilated_out = jnp.zeros(
        (2 * position_count, HALF_WINDOW_ROWS, kernel_low.shape[2]), jnp.float32
    )
    for kernel_tap_index in range(3):
        displaced_rows = entry_widened[
            :,
            kernel_tap_index * DILATION_STEP : kernel_tap_index * DILATION_STEP + HALF_WINDOW_ROWS,
        ]
        dilated_out = dilated_out + jnp.einsum(
            "hrc,cf->hrf",
            displaced_rows,
            kernel_low[kernel_tap_index],
            preferred_element_type=jnp.float32,
        )
    dilated_out = dilated_out.reshape(position_count, WINDOW_SPAN, -1)
    middle_centre, middle_scale = moments(dilated_out, valid_mask, row_count)
    middle_norm = (dilated_out - middle_centre) * middle_scale
    middle_smooth, middle_back = jax.vjp(smooth, middle_norm * middle_gain + middle_shift)
    middle_act = (middle_smooth * valid_mask).astype(jnp.bfloat16)
    pointwise_low = pointwise_kernel.astype(jnp.bfloat16)
    mixed_out = jnp.einsum(
        "krf,fd->krd", middle_act, pointwise_low, preferred_element_type=jnp.float32
    )
    activations = (valid_mask * (pooled + mixed_out + pointwise_bias)).reshape(-1, channel_width)
    grad_block = cotangent.reshape(position_count, WINDOW_SPAN, channel_width) * valid_mask
    grad_mixed = grad_block.astype(jnp.bfloat16)
    bias_part = jnp.sum(grad_block, axis=(0, 1))
    pointwise_part = jnp.einsum(
        "krf,krd->fd", middle_act, grad_mixed, preferred_element_type=jnp.float32
    )
    grad_middle = jnp.einsum(
        "krd,fd->krf", grad_mixed, pointwise_low, preferred_element_type=jnp.float32
    )
    grad_middle_pre = middle_back(grad_middle * valid_mask)[0]
    middle_gain_part = jnp.sum(grad_middle_pre * middle_norm, axis=(0, 1))
    middle_shift_part = jnp.sum(grad_middle_pre, axis=(0, 1))
    (
        middle_gain_gradient,
        middle_shift_gradient,
        pointwise_kernel_gradient,
        pointwise_bias_gradient,
    ) = lax.psum((middle_gain_part, middle_shift_part, pointwise_part, bias_part), ("grp", "seq"))
    dilated_gradient = (
        middle_gain
        * middle_scale
        * (
            grad_middle_pre
            - (middle_shift_gradient + middle_norm * middle_gain_gradient) / row_count
        )
        * valid_mask
    )
    dilated_gradient = dilated_gradient.astype(jnp.bfloat16)
    border_gradient = from_partner(
        dilated_gradient[:, HALF_WINDOW_ROWS - DILATION_STEP : HALF_WINDOW_ROWS + DILATION_STEP],
        "seq",
        0,
    )
    grad_wide = extended(dilated_gradient, border_gradient)
    grad_halves = dilated_gradient.reshape(2 * position_count, HALF_WINDOW_ROWS, -1)
    kernel_pieces = []
    grad_entry = jnp.zeros((2 * position_count, HALF_WINDOW_ROWS, channel_width), jnp.float32)
    for kernel_tap_index in range(3):
        displaced_rows = entry_widened[
            :,
            kernel_tap_index * DILATION_STEP : kernel_tap_index * DILATION_STEP + HALF_WINDOW_ROWS,
        ]
        kernel_pieces.append(
            jnp.einsum(
                "hrc,hrf->cf", displaced_rows, grad_halves, preferred_element_type=jnp.float32
            )
        )
        backward_offset = (2 - kernel_tap_index) * DILATION_STEP
        grad_shifted = grad_wide[:, backward_offset : backward_offset + HALF_WINDOW_ROWS]
        grad_entry = grad_entry + jnp.einsum(
            "hrf,cf->hrc",
            grad_shifted,
            kernel_low[kernel_tap_index],
            preferred_element_type=jnp.float32,
        )
    kernel_part = jnp.stack(kernel_pieces)
    grad_entry = grad_entry.reshape(position_count, WINDOW_SPAN, channel_width)
    grad_entry_pre = entry_back(grad_entry * valid_mask)[0]
    entry_gain_part = jnp.sum(grad_entry_pre * entry_norm, axis=(0, 1))
    entry_shift_part = jnp.sum(grad_entry_pre, axis=(0, 1))
    entry_gain_gradient, entry_shift_gradient, dilated_kernel_gradient = lax.psum(
        (entry_gain_part, entry_shift_part, kernel_part), ("grp", "seq")
    )
    grad_pooled = (
        entry_gain
        * entry_scale
        * (grad_entry_pre - (entry_shift_gradient + entry_norm * entry_gain_gradient) / row_count)
        * valid_mask
        + grad_block
    )
    returned = lax.all_to_all(
        grad_pooled.astype(jnp.bfloat16), "seq", split_axis=1, concat_axis=0, tiled=True
    )
    inverse = (
        jnp.zeros((group_windows,), jnp.int32)
        .at[picked]
        .set(jnp.arange(group_windows, dtype=jnp.int32))
    )
    grad_source = jnp.take(returned, inverse, axis=0).astype(jnp.float32) * source_valid
    zero_part = jnp.zeros_like(grad_source)
    signal_gradient = jnp.stack(
        [
            jnp.where(take_first, grad_source, zero_part),
            jnp.where(take_first, zero_part, grad_source),
        ],
        axis=2,
    ).reshape(group_windows, segment, channel_width)
    return (
        activations,
        signal_gradient,
        entry_gain_gradient,
        entry_shift_gradient,
        dilated_kernel_gradient,
        middle_gain_gradient,
        middle_shift_gradient,
        pointwise_kernel_gradient,
        pointwise_bias_gradient,
    )


def solution(mesh):
    return jax.shard_map(
        per_device,
        mesh=mesh,
        in_specs=(
            P("grp", "seq", None),
            P(),
            P(),
            P(),
            P(),
            P(),
            P(),
            P(),
            P(),
            P("grp", None),
            P(("grp", "seq"), None),
        ),
        out_specs=(
            P(("grp", "seq"), None),
            P("grp", "seq", None),
            P(),
            P(),
            P(),
            P(),
            P(),
            P(),
            P(),
        ),
        check_vma=False,
    )
```

profile of v0, /device:TPU:0, one launch (start us, length us, event | category | flops | bytes accessed | tf_op | source)
XLA Modules:
  0.0 660.3 jit_solution(9878125855591612174)
XLA Ops:
  8.7 16.6 %copy.79 = f32[16,256,768]{2,0,1:T(8,128)} copy(f32[16,256,768]{2,1,0:T(8,128)} %param.15) | data formatting | bytes 25165824 | tf_op args[0]
  25.4 10.5 %fusion.86 = (f32[16,128,1,768]{3,0,2,1:T(8,128)}, f32[16,128,1,768]{3,0,2,1:T(8,128)}) fusion(f32[16,128,2,768]{3,0,2,1:T(8,128)} %bitcast.168), kind=kLoop, calls=%fused_computation.166 | loop fusion | bytes 25165824 | tf_op jit(solution)/shard_map/slice | solution.py:71
  36.1 11.7 %multiply_convert_fusion.1 = (bf16[16,128,768]{2,1,0:T(8,128)(2,1)}, pred[16,128,768]{2,1,0:T(8,128)(4,1)}) fusion(f32[16,128,1,768]{3,0,2,1:T(8,128)} %get-tuple-element.66, f32[16,128,1,768]{3,0,2,1:T(8,128)} %get-tuple-element.65, f32[16,128]{1,0:T(8,128)S(1)} %compare_convert_fusion.2), kind=kLoop, calls=%fused_computation.48 | loop fusion | flops 6291456 | bytes 17309696 | tf_op jit(solution)/shard_map/convert_element_type | solution.py:78
  47.8 2.6 gather_fusion.3
  50.4 2.0 broadcast_select_fusion.1
  52.4 7.4 %all-to-all-start = ((bf16[16,128,768]{2,1,0:T(8,128)(2,1)}), bf16[16,128,768]{2,1,0:T(8,128)(2,1)S(1)}, u32[]{:S(2)}, u32[]{:S(2)}) async-start(bf16[16,128,768]{2,1,0:T(8,128)(2,1)} %broadcast_select_fusion.1), calls=%async_computation | async-start | bytes 6291456 | tf_op jit(solution)/shard_map/all_to_all | solution.py:89
  61.7 3.7 convert_element_type.105
  66.3 5.2 multiply_convert_fusion.2
  71.5 3.5 fusion.38
  75.1 55.5 %all-to-all-done = bf16[16,128,768]{2,1,0:T(8,128)(2,1)S(1)} async-done(((bf16[16,128,768]{2,1,0:T(8,128)(2,1)}), bf16[16,128,768]{2,1,0:T(8,128)(2,1)S(1)}, u32[]{:S(2)}, u32[]{:S(2)}) %all-to-all-start) | async-done | bytes 3145760 | tf_op jit(solution)/shard_map/all_to_all | solution.py:89
  131.3 37.8 %psum.77 = f32[768]{0:T(1024)S(1)} all-reduce(f32[768]{0:T(1024)S(1)} %multiply_reduce_fusion.2), channel_id=1, replica_groups=mesh['grp'=4,'seq'=8] {'grp','seq'}, use_global_device_ids=true, to_apply=%region_1.4 | all-reduce | flops 768 | bytes 6144 | tf_op jit(solution)/shard_map/psum | solution.py:27
  170.8 41.7 %psum.78 = f32[768]{0:T(1024)S(1)} all-reduce(f32[768]{0:T(1024)S(1)} %multiply_reduce_fusion.1), channel_id=1, replica_groups=mesh['grp'=4,'seq'=8] {'grp','seq'}, use_global_device_ids=true, to_apply=%region_4.7 | all-reduce | flops 768 | bytes 6144 | tf_op jit(solution)/shard_map/psum | solution.py:29
  214.6 3.4 multiply_convert_fusion
  218.1 2.3 collective-permute-start
  220.6 4.9 collective-permute-done
  227.3 1.9 copy-done.10
  229.2 1.8 fusion.43
  231.0 1.8 fusion.51
  232.9 2.0 multiply_reduce_fusion.6
  234.9 38.2 %psum.79 = f32[384]{0:T(512)S(1)} all-reduce(f32[384]{0:T(512)S(1)} %get-tuple-element.86), channel_id=1, replica_groups=mesh['grp'=4,'seq'=8] {'grp','seq'}, use_global_device_ids=true, to_apply=%region_6.9 | all-reduce | flops 384 | bytes 3072 | tf_op jit(solution)/shard_map/psum | solution.py:27
  274.2 41.7 %psum.80 = f32[384]{0:T(512)S(1)} all-reduce(f32[384]{0:T(512)S(1)} %multiply_reduce_fusion.5), channel_id=1, replica_groups=mesh['grp'=4,'seq'=8] {'grp','seq'}, use_global_device_ids=true, to_apply=%region_8.11 | all-reduce | flops 384 | bytes 3072 | tf_op jit(solution)/shard_map/psum | solution.py:29
  316.6 6.1 fusion.81
  322.7 38.7 %all-reduce.1 = (f32[384]{0:T(512)S(1)}, f32[384]{0:T(512)S(1)}) all-reduce(f32[384]{0:T(512)S(1)} %get-tuple-element.50, f32[384]{0:T(512)S(1)} %get-tuple-element.49), channel_id=1, replica_groups=mesh['grp'=4,'seq'=8] {'grp','seq'}, use_global_device_ids=true, to_apply=%region_12.15 | all-reduce | flops 768 | bytes 6144 | tf_op jit(solution)/shard_map/psum | solution.py:156
  361.4 3.0 multiply_convert_fusion.5
  364.5 2.3 collective-permute-start.1
  367.0 2.7 collective-permute-done.1
  371.6 1.8 fusion.56
  373.5 1.8 fusion.58
  375.3 8.2 %fusion.80 = (f32[768]{0:T(1024)S(1)}, f32[768]{0:T(1024)S(1)}, f32[4,512,768]{2,1,0:T(8,128)}) fusion(f32[768]{0:T(1024)S(1)} %get-tuple-element.59, f32[4,512,768]{2,1,0:T(8,128)S(1)} %bitcast.163, f32[768]{0:T(1024)S(1)} %broadcast_divide_fusion, f32[768]{0:T(1024)S(1)} %copy-done.15, f32[768]{0:T(1024)S(1)} %copy-done.13, f32[4,512]{1,0:T(4,128)S(1)} %fusion.74, ...), kind=kOutput, calls=%fused_computation.162 | convolution fusion | flops 1253571072 | bytes 27359232 | tf_op jit(solution)/shard_map/hrf,cf->hrc/dot_general | solution.py:188
  383.5 41.3 %all-reduce = (f32[768]{0:T(1024)S(1)}, f32[768]{0:T(1024)S(1)}, f32[768]{0:T(1024)}) all-reduce(f32[768]{0:T(1024)S(1)} %get-tuple-element.48, f32[768]{0:T(1024)S(1)} %get-tuple-element.47, f32[768]{0:T(1024)S(1)} %get-tuple-element.68), channel_id=1, replica_groups=mesh['grp'=4,'seq'=8] {'grp','seq'}, use_global_device_ids=true, to_apply=%region_16.19 | all-reduce | flops 2304 | bytes 18432 | tf_op jit(solution)/shard_map/psum | solution.py:199
  424.8 11.1 %fusion.10 = bf16[2,1024,768]{2,1,0:T(8,128)(2,1)S(1)} fusion(f32[2,1024,768]{2,1,0:T(8,128)} %bitcast.164, f32[2,8,128,768]{3,2,1,0:T(8,128)} %copy-done.1, f32[]{:T(128)} %convert_reduce_fusion, f32[768]{0:T(1024)S(1)} %get-tuple-element.95, f32[768]{0:T(1024)S(1)} %get-tuple-element.96, f32[768]{0:T(1024)S(1)} %get-tuple-element.58, ...), kind=kLoop, calls=%fused_computation.21 | loop fusion | flops 51904512 | bytes 22049796 | tf_op jit(solution)/shard_map/convert_element_type | solution.py:210
  435.9 5.0 copy.86
  440.9 5.2 all-to-all-start.1
  446.2 4.3 fusion.60
  450.5 1.8 fusion.66
  452.3 1.8 fusion.63
  454.2 2.0 pad_maximum_fusion.2
  458.1 2.4 convolution_bitcast_fusion
  462.3 7.3 %fusion.19 = f32[2,1024,768]{2,1,0:T(8,128)} fusion(f32[2,8,128,768]{3,2,1,0:T(8,128)} %copy-done.1, f32[768]{0:T(1024)S(1)} %copy-done.17, f32[2,1024]{1,0:T(2,128)S(1)} %compare_convert_fusion.1, bf16[2,1024,384]{2,1,0:T(8,128)(2,1)S(1)} %copy-done.5, f32[384,768]{1,0:T(8,128)S(1)} %copy-done.7), kind=kOutput, calls=%fused_computation.36 | convolution fusion | flops 1212973056 | bytes 15346688 | tf_op jit(solution)/shard_map/krf,fd->krd/dot_general | solution.py:135
  469.6 68.6 %all-to-all-done.1 = bf16[2,1024,768]{2,0,1:T(2,128)(2,1)} async-done(((bf16[2,1024,768]{2,0,1:T(2,128)(2,1)}), bf16[2,1024,768]{2,0,1:T(2,128)(2,1)}, u32[]{:S(2)}, u32[]{:S(2)}) %all-to-all-start.1) | async-done | bytes 3145760 | tf_op jit(solution)/shard_map/all_to_all | solution.py:209
  538.2 2.3 copy.87
  540.7 2.4 gather_fusion.4
  543.1 5.3 select_bitcast_fusion.1
  548.4 9.2 %pad_maximum_fusion = f32[16,128,2,768]{3,1,0,2:T(8,128)} fusion(f32[16,128,1,768]{3,1,0,2:T(8,128)} %get-tuple-element.70, f32[16,128,1,768]{3,1,0,2:T(8,128)S(1)} %get-tuple-element.69), kind=kLoop, calls=%fused_computation.6 | loop fusion | flops 3145728 | bytes 25165824 | tf_op jit(solution)/shard_map/stack | solution.py:219
  557.6 16.5 %copy.89 = f32[16,128,2,768]{3,0,2,1:T(8,128)} copy(f32[16,128,2,768]{3,1,0,2:T(8,128)} %pad_maximum_fusion) | data formatting | bytes 25165824 | tf_op jit(solution)/shard_map/stack | solution.py:219
  574.0 16.9 %copy.94 = f32[16,256,768]{2,1,0:T(8,128)} copy(f32[16,256,768]{2,0,1:T(8,128)} %bitcast.169) | data formatting | bytes 25165824
  590.9 57.0 %all-reduce.5.cloned.1.call-done = (f32[3,768,384]{2,1,0:T(8,128)}, f32[384,768]{1,0:T(8,128)}) async-done(((f32[3,768,384]{2,1,0:T(8,128)}, f32[384,768]{1,0:T(8,128)}), (f32[3,768,384]{2,1,0:T(8,128)}, f32[384,768]{1,0:T(8,128)})) %all-reduce.5.cloned.1.call-update) | async-done | bytes 4718608 | tf_op jit(solution)/shard_map/psum | solution.py:199
  647.9 4.1 copy.127
  (128 shorter events, 19.6 us)
Async XLA Ops:
  25.4 10.5 %copy-start.22 = (s32[64]{0:T(128)S(1)}, s32[64]{0:T(128)}, u32[]{:S(2)}) copy-start(s32[64]{0:T(128)} %param.23) | copy-start | bytes 772
  52.4 7.5 %copy-start = (s32[1,16]{1,0:T(1,128)S(1)}, s32[1,16]{1,0:T(1,128)}, u32[]{:S(2)}) copy-start(s32[1,16]{1,0:T(1,128)} %param.24) | copy-start | bytes 196
  52.4 78.1 %all-to-all-start = ((bf16[16,128,768]{2,1,0:T(8,128)(2,1)}), bf16[16,128,768]{2,1,0:T(8,128)(2,1)S(1)}, u32[]{:S(2)}, u32[]{:S(2)}) async-start(bf16[16,128,768]{2,1,0:T(8,128)(2,1)} %broadcast_select_fusion.1), calls=%async_computation | async-start | bytes 6291456 | tf_op jit(solution)/shard_map/all_to_all | solution.py:89
  61.7 9.9 %slice-start.2 = ((s8[6291456]{0:T(1024)(128)(4,1)}), s8[4194304]{0:T(1024)(128)(4,1)S(1)}, s32[]{:S(2)}) async-start(s8[6291456]{0:T(1024)(128)(4,1)} %bitcast.165), calls=%async_computation.5 | async-start | bytes 8388608
  66.3 5.2 slice-start.3
  66.3 5.2 copy-start.6
  213.2 0.7 copy-start.13
  213.2 1.3 copy-start.15
  213.9 4.1 copy-start.1
  218.1 7.4 %collective-permute-start = (bf16[2,76,768]{2,1,0:T(8,128)(2,1)S(1)}, bf16[2,76,768]{2,1,0:T(8,128)(2,1)S(1)}, u32[]{:S(2)}, u32[]{:S(2)}) collective-permute-start(bf16[2,76,768]{2,1,0:T(8,128)(2,1)S(1)} %slice.103), channel_id=1, source_target_pairs={{0,1},{1,0},{2,3},{3,2},{4,5},{5,4},{6,7},{7,6},{8,9},{9,8},{10,11... | collective-permute-start | bytes 700424 | tf_op jit(solution)/shard_map/ppermute | solution.py:19
  227.0 2.1 copy-start.10
  227.3 5.6 copy-start.8
  234.9 81.1 %copy-start.14 = (f32[384]{0:T(512)S(1)}, f32[384]{0:T(512)}, u32[]{:S(2)}) copy-start(f32[384]{0:T(512)} %param.19) | copy-start | bytes 4612
  234.9 81.7 %copy-start.16 = (f32[384]{0:T(512)S(1)}, f32[384]{0:T(512)}, u32[]{:S(2)}) copy-start(f32[384]{0:T(512)} %param.20) | copy-start | bytes 4612
  361.4 3.1 copy-start.20
  361.4 3.1 copy-start.21
  364.4 2.4 copy-start.3
  364.5 5.2 collective-permute-start.1
  370.2 1.5 copy-start.11
  370.4 4.9 slice-start
  371.6 3.7 slice-start.1
  424.8 11.1 %copy-start.18 = (f32[768]{0:T(1024)}, f32[768]{0:T(1024)S(1)}, u32[]{:S(2)}) copy-start(f32[768]{0:T(1024)S(1)} %get-tuple-element.95) | copy-start | bytes 9220
  424.8 11.1 %copy-start.19 = (f32[768]{0:T(1024)}, f32[768]{0:T(1024)S(1)}, u32[]{:S(2)}) copy-start(f32[768]{0:T(1024)S(1)} %get-tuple-element.96) | copy-start | bytes 9220
  440.9 97.2 %all-to-all-start.1 = ((bf16[2,1024,768]{2,0,1:T(2,128)(2,1)}), bf16[2,1024,768]{2,0,1:T(2,128)(2,1)}, u32[]{:S(2)}, u32[]{:S(2)}) async-start(bf16[2,1024,768]{2,0,1:T(2,128)(2,1)} %copy.86), calls=%async_computation.1 | async-start | bytes 6291456 | tf_op jit(solution)/shard_map/all_to_all | solution.py:209
  446.1 201.8 %all-reduce.5.cloned.1.call-start = ((), (), s32[]{:S(2)}) async-start(), calls=%async_computation.2 | async-start | bytes 9437184 | tf_op jit(solution)/shard_map/psum | solution.py:199
  446.2 4.3 copy-start.4
  446.2 4.3 copy-start.9
  456.2 1.9 copy-start.2
  460.5 1.4 copy-start.5
  460.5 1.7 copy-start.7
  460.5 1.7 copy-start.17
  647.9 4.1 copy-start.12
Sparse Core Ops, SparseCore 0:
  460.7 187.1 all-reduce.4
where the time goes:
time: 668 us; the launch traced here: 660 us
  blocking collectives  239 us (36%)
  waiting for transfers between devices  189 us (28%)
  local copies, waits for them, and re-layouts  88.1 us (13%)
  other arithmetic  73 us (11%)
  matrix products  38.7 us (6%)
  starting transfers between devices  17.3 us (3%)
  between operations  15.1 us (2%)
    psum x2, blocking collectives, moments(): lax.psum(jnp.sum(deviation * deviation, axis=(0, 1)), ('grp', 'seq'))  83.4 us
    psum x2, blocking collectives, moments(): lax.psum(jnp.sum(values * valid_mask, axis=(0, 1)), ('grp', 'seq'))  76 us
    all_to_all x1, waiting for transfers between devices, per_device(): lax.all_to_all(grad_pooled.astype(jnp.bfloat16), 'seq', split_axis=1, con...  68.6 us
    psum x1, waiting for transfers between devices, per_device(): lax.psum((entry_gain_part, entry_shift_part, kernel_part), ('grp', 'seq'))  57 us
    all_to_all x1, waiting for transfers between devices, per_device(): lax.all_to_all(outgoing, 'seq', split_axis=0, concat_axis=1, tiled=True)  55.5 us
    unnamed x61, local copies, waits for them, and re-layouts  43.3 us
    psum x1, blocking collectives, per_device(): lax.psum((entry_gain_part, entry_shift_part, kernel_part), ('grp', 'seq'))  41.3 us
    psum x1, blocking collectives, per_device(): lax.psum((middle_gain_part, middle_shift_part, pointwise_part, bias_part)...  38.7 us
  transfers between devices with their start and end apart: 5, of which 5 were waited for; matrix products, arithmetic and copies ran while one was open for 14% of the time, Pallas kernels for 0%

commit v1 on v0

--- a/solution.py
+++ b/solution.py
@@ -7,6 +7,11 @@
 WINDOW_SPAN = 1024
 HALF_WINDOW_ROWS = 512
 EPSILON = 0.001
+
+
+def by_each_axis(x, inner_axis, outer_axis):
+    partial = lax.psum(x, inner_axis)
+    return lax.psum(partial, outer_axis)
 
 
 def from_partner(block, axis, bit):
@@ -196,8 +201,8 @@
     grad_entry_pre = entry_back(grad_entry * valid_mask)[0]
     entry_gain_part = jnp.sum(grad_entry_pre * entry_norm, axis=(0, 1))
     entry_shift_part = jnp.sum(grad_entry_pre, axis=(0, 1))
-    entry_gain_gradient, entry_shift_gradient, dilated_kernel_gradient = lax.psum(
-        (entry_gain_part, entry_shift_part, kernel_part), ("grp", "seq")
+    entry_gain_gradient, entry_shift_gradient, dilated_kernel_gradient = by_each_axis(
+        (entry_gain_part, entry_shift_part, kernel_part), "seq", "grp"
     )
     grad_pooled = (
         entry_gain

time: 668 us -> 865 us (1.29)
  waiting for transfers between devices: 189 us -> 398 us
  blocking collectives: 239 us -> 225 us
    psum x1 -> x3, waiting for transfers between devices: 57 us -> 335 us  [the longest x1 182 us: by_each_axis(): partial = lax.psum(x, inner_axis)]
    all_to_all x1, waiting for transfers between devices: 68.6 us -> 0.01 us  [per_device(): lax.all_to_all(grad_pooled.astype(jnp.bfloat16), 'seq', split_axis=1, con...]
    psum x1 -> x2, blocking collectives: 41.3 us -> 26.7 us  [the longest x1 20.9 us: by_each_axis(): partial = lax.psum(x, inner_axis)]
    unnamed x61 -> x63, local copies, waits for them, and re-layouts: 43.3 us -> 42.3 us
  transfers between devices with their start and end apart: 5 -> 7, of which waited for: 5 -> 6; matrix products, arithmetic and copies ran while one was open for 14% -> 10% of each run, Pallas kernels for 0% -> 0%
where the time goes in v1:
time: 865 us; the launch traced here: 857 us
  waiting for transfers between devices  398 us (46%)
  blocking collectives  225 us (26%)
  local copies, waits for them, and re-layouts  87 us (10%)
  other arithmetic  73.9 us (9%)
  matrix products  40.8 us (5%)
  starting transfers between devices  16.9 us (2%)
  between operations  14.9 us (2%)
    psum x1, waiting for transfers between devices, by_each_axis(): partial = lax.psum(x, inner_axis)  182 us
    psum x2, blocking collectives, moments(): lax.psum(jnp.sum(deviation * deviation, axis=(0, 1)), ('grp', 'seq'))  83.5 us
    psum x1, waiting for transfers between devices, per_device(): lax.psum((middle_gain_part, middle_shift_part, pointwise_part, bias_part)...  76.8 us
    psum x1, waiting for transfers between devices, by_each_axis(): return lax.psum(partial, outer_axis)  76.2 us
    psum x2, blocking collectives, moments(): lax.psum(jnp.sum(values * valid_mask, axis=(0, 1)), ('grp', 'seq'))  76 us
    all_to_all x1, waiting for transfers between devices, per_device(): lax.all_to_all(outgoing, 'seq', split_axis=0, concat_axis=1, tiled=True)  55.5 us
    unnamed x63, local copies, waits for them, and re-layouts  42.3 us
    psum x1, blocking collectives, per_device(): lax.psum((middle_gain_part, middle_shift_part, pointwise_part, bias_part)...  38.8 us
  transfers between devices with their start and end apart: 7, of which 6 were waited for; matrix products, arithmetic and copies ran while one was open for 10% of the time, Pallas kernels for 0%

profile of v1, /device:TPU:0, one launch (start us, length us, event | category | flops | bytes accessed | tf_op | source)
XLA Modules:
  0.0 856.6 jit_solution(8497132600829119011)
XLA Ops:
  8.7 16.6 %copy.79 = f32[16,256,768]{2,0,1:T(8,128)} copy(f32[16,256,768]{2,1,0:T(8,128)} %param.15) | data formatting | bytes 25165824 | tf_op args[0]
  25.4 10.6 %fusion.86 = (f32[16,128,1,768]{3,0,2,1:T(8,128)}, f32[16,128,1,768]{3,0,2,1:T(8,128)}) fusion(f32[16,128,2,768]{3,0,2,1:T(8,128)} %bitcast.168), kind=kLoop, calls=%fused_computation.166 | loop fusion | bytes 25165824 | tf_op jit(solution)/shard_map/slice | solution.py:76
  36.1 11.7 %multiply_convert_fusion.1 = (bf16[16,128,768]{2,1,0:T(8,128)(2,1)}, pred[16,128,768]{2,1,0:T(8,128)(4,1)}) fusion(f32[16,128,1,768]{3,0,2,1:T(8,128)} %get-tuple-element.66, f32[16,128,1,768]{3,0,2,1:T(8,128)} %get-tuple-element.65, f32[16,128]{1,0:T(8,128)S(1)} %compare_convert_fusion.2), kind=kLoop, calls=%fused_computation.48 | loop fusion | flops 6291456 | bytes 17309696 | tf_op jit(solution)/shard_map/convert_element_type | solution.py:83
  47.8 2.6 gather_fusion.3
  50.4 2.0 broadcast_select_fusion.1
  52.5 7.4 all-to-all-start
  61.7 3.5 convert_element_type.105
  66.3 5.2 multiply_convert_fusion.2
  71.6 3.5 fusion.38
  75.1 55.5 %all-to-all-done = bf16[16,128,768]{2,1,0:T(8,128)(2,1)S(1)} async-done(((bf16[16,128,768]{2,1,0:T(8,128)(2,1)}), bf16[16,128,768]{2,1,0:T(8,128)(2,1)S(1)}, u32[]{:S(2)}, u32[]{:S(2)}) %all-to-all-start) | async-done | bytes 3145760 | tf_op jit(solution)/shard_map/all_to_all | solution.py:94
  131.3 37.9 %psum.98 = f32[768]{0:T(1024)S(1)} all-reduce(f32[768]{0:T(1024)S(1)} %multiply_reduce_fusion.2), channel_id=1, replica_groups=mesh['grp'=4,'seq'=8] {'grp','seq'}, use_global_device_ids=true, to_apply=%region_1.4 | all-reduce | flops 768 | bytes 6144 | tf_op jit(solution)/shard_map/psum | solution.py:32
  170.9 41.7 %psum.99 = f32[768]{0:T(1024)S(1)} all-reduce(f32[768]{0:T(1024)S(1)} %multiply_reduce_fusion.1), channel_id=1, replica_groups=mesh['grp'=4,'seq'=8] {'grp','seq'}, use_global_device_ids=true, to_apply=%region_4.7 | all-reduce | flops 768 | bytes 6144 | tf_op jit(solution)/shard_map/psum | solution.py:34
  214.7 3.4 multiply_convert_fusion
  218.2 2.3 collective-permute-start
  220.8 4.9 collective-permute-done
  227.4 1.9 copy-done.9
  229.3 1.8 fusion.43
  233.0 2.0 multiply_reduce_fusion.6
  235.0 38.2 %psum.100 = f32[384]{0:T(512)S(1)} all-reduce(f32[384]{0:T(512)S(1)} %get-tuple-element.86), channel_id=1, replica_groups=mesh['grp'=4,'seq'=8] {'grp','seq'}, use_global_device_ids=true, to_apply=%region_6.9 | all-reduce | flops 384 | bytes 3072 | tf_op jit(solution)/shard_map/psum | solution.py:32
  274.4 41.8 %psum.101 = f32[384]{0:T(512)S(1)} all-reduce(f32[384]{0:T(512)S(1)} %multiply_reduce_fusion.5), channel_id=1, replica_groups=mesh['grp'=4,'seq'=8] {'grp','seq'}, use_global_device_ids=true, to_apply=%region_8.11 | all-reduce | flops 384 | bytes 3072 | tf_op jit(solution)/shard_map/psum | solution.py:34
  316.8 6.1 fusion.81
  322.9 38.8 %all-reduce = (f32[384]{0:T(512)S(1)}, f32[384]{0:T(512)S(1)}, f32[768]{0:T(1024)}) all-reduce(f32[384]{0:T(512)S(1)} %get-tuple-element.50, f32[384]{0:T(512)S(1)} %get-tuple-element.49, f32[768]{0:T(1024)S(1)} %get-tuple-element.68), channel_id=1, replica_groups=mesh['grp'=4,'seq'=8] {'grp','seq'}, use_global_device_ids=true, to_apply=%region_12.15 | all-reduce | flops 1536 | bytes 12288 | tf_op jit(solution)/shard_map/psum | solution.py:161
  361.7 3.4 multiply_convert_fusion.5
  365.2 2.8 fusion.66
  368.1 2.9 fusion.63
  370.9 2.6 collective-permute-start.1
  373.7 2.7 collective-permute-done.1
  380.2 1.8 fusion.58
  382.0 8.2 fusion.80
  390.2 20.9 %all-reduce.1 = (f32[768]{0:T(1024)S(1)}, f32[768]{0:T(1024)S(1)}) all-reduce(f32[768]{0:T(1024)S(1)} %get-tuple-element.48, f32[768]{0:T(1024)S(1)} %get-tuple-element.47), channel_id=1, replica_groups=mesh['grp'=4,'seq'=8] {'seq'}, use_global_device_ids=true, to_apply=%region_17.20 | all-reduce | flops 1536 | bytes 12288 | tf_op jit(solution)/shard_map/psum | solution.py:13
  411.1 5.8 all-reduce.2
  416.9 11.3 %fusion.10 = bf16[2,1024,768]{2,1,0:T(8,128)(2,1)S(1)} fusion(f32[2,1024,768]{2,1,0:T(8,128)} %bitcast.164, f32[2,8,128,768]{3,2,1,0:T(8,128)} %copy-done.1, f32[]{:T(128)} %convert_reduce_fusion, f32[768]{0:T(1024)S(1)} %get-tuple-element.95, f32[768]{0:T(1024)S(1)} %get-tuple-element.96, f32[768]{0:T(1024)S(1)} %get-tuple-element.58, ...), kind=kLoop, calls=%fused_computation.21 | loop fusion | flops 51904512 | bytes 22049796 | tf_op jit(solution)/shard_map/convert_element_type | solution.py:215
  428.3 4.8 copy.86
  433.1 4.4 all-to-all-start.1
  437.6 4.3 fusion.60
  442.0 2.0 pad_maximum_fusion.2
  446.0 2.4 convolution_bitcast_fusion
  449.2 182.1 %all-reduce.7.cloned.1.call-done = f32[3,768,384]{2,1,0:T(8,128)} async-done(((f32[3,768,384]{2,1,0:T(8,128)}), f32[3,768,384]{2,1,0:T(8,128)}) %all-reduce.7.cloned.1.call-update) | async-done | bytes 3538960 | tf_op jit(solution)/shard_map/psum | solution.py:13
  631.4 7.3 fusion.19
  638.7 2.3 copy.87
  641.2 2.4 gather_fusion.4
  643.6 5.3 select_bitcast_fusion.1
  648.9 9.2 %pad_maximum_fusion = f32[16,128,2,768]{3,1,0,2:T(8,128)} fusion(f32[16,128,1,768]{3,1,0,2:T(8,128)} %get-tuple-element.70, f32[16,128,1,768]{3,1,0,2:T(8,128)S(1)} %get-tuple-element.69), kind=kLoop, calls=%fused_computation.6 | loop fusion | flops 3145728 | bytes 25165824 | tf_op jit(solution)/shard_map/stack | solution.py:224
  658.1 16.4 %copy.89 = f32[16,128,2,768]{3,0,2,1:T(8,128)} copy(f32[16,128,2,768]{3,1,0,2:T(8,128)} %pad_maximum_fusion) | data formatting | bytes 25165824 | tf_op jit(solution)/shard_map/stack | solution.py:224
  674.5 16.9 %copy.94 = f32[16,256,768]{2,1,0:T(8,128)} copy(f32[16,256,768]{2,0,1:T(8,128)} %bitcast.169) | data formatting | bytes 25165824
  691.5 76.8 %all-reduce.11.cloned.1.call-done = f32[384,768]{1,0:T(8,128)} async-done(((f32[384,768]{1,0:T(8,128)}), f32[384,768]{1,0:T(8,128)}) %all-reduce.11.cloned.1.call-update) | async-done | bytes 1179664 | tf_op jit(solution)/shard_map/psum | solution.py:161
  768.3 76.2 %all-reduce.9.cloned.1.call-done = f32[3,768,384]{2,1,0:T(8,128)} async-done(((f32[3,768,384]{2,1,0:T(8,128)}), f32[3,768,384]{2,1,0:T(8,128)}) %all-reduce.9.cloned.1.call-update) | async-done | bytes 3538960 | tf_op jit(solution)/shard_map/psum | solution.py:14
  844.5 4.1 copy.128
  (137 shorter events, 22.6 us)
Async XLA Ops:
  25.4 10.6 %copy-start.23 = (s32[64]{0:T(128)S(1)}, s32[64]{0:T(128)}, u32[]{:S(2)}) copy-start(s32[64]{0:T(128)} %param.23) | copy-start | bytes 772
  52.5 7.5 copy-start
  52.5 78.1 %all-to-all-start = ((bf16[16,128,768]{2,1,0:T(8,128)(2,1)}), bf16[16,128,768]{2,1,0:T(8,128)(2,1)S(1)}, u32[]{:S(2)}, u32[]{:S(2)}) async-start(bf16[16,128,768]{2,1,0:T(8,128)(2,1)} %broadcast_select_fusion.1), calls=%async_computation | async-start | bytes 6291456 | tf_op jit(solution)/shard_map/all_to_all | solution.py:94
  61.7 9.9 %slice-start.2 = ((s8[6291456]{0:T(1024)(128)(4,1)}), s8[4194304]{0:T(1024)(128)(4,1)S(1)}, s32[]{:S(2)}) async-start(s8[6291456]{0:T(1024)(128)(4,1)} %bitcast.165), calls=%async_computation.7 | async-start | bytes 8388608
  66.3 5.3 slice-start.3
  66.3 5.3 copy-start.5
  213.3 0.7 copy-start.14
  213.3 1.4 copy-start.16
  214.0 4.2 copy-start.1
  218.2 7.4 collective-permute-start
  227.2 2.1 copy-start.9
  227.4 5.5 copy-start.7
  235.0 81.1 %copy-start.15 = (f32[384]{0:T(512)S(1)}, f32[384]{0:T(512)}, u32[]{:S(2)}) copy-start(f32[384]{0:T(512)} %param.19) | copy-start | bytes 4612
  235.0 81.8 %copy-start.17 = (f32[384]{0:T(512)S(1)}, f32[384]{0:T(512)}, u32[]{:S(2)}) copy-start(f32[384]{0:T(512)} %param.20) | copy-start | bytes 4612
  361.7 3.4 copy-start.21
  361.7 3.5 copy-start.22
  361.7 3.5 copy-start.8
  365.2 8.3 copy-start.3
  370.9 5.4 collective-permute-start.1
  376.9 1.5 copy-start.10
  377.1 4.9 slice-start
  378.3 3.7 slice-start.1
  416.9 11.3 %copy-start.19 = (f32[768]{0:T(1024)}, f32[768]{0:T(1024)S(1)}, u32[]{:S(2)}) copy-start(f32[768]{0:T(1024)S(1)} %get-tuple-element.95) | copy-start | bytes 9220
  416.9 11.3 %copy-start.20 = (f32[768]{0:T(1024)}, f32[768]{0:T(1024)S(1)}, u32[]{:S(2)}) copy-start(f32[768]{0:T(1024)S(1)} %get-tuple-element.96) | copy-start | bytes 9220
  433.1 205.6 %all-to-all-start.1 = ((bf16[2,1024,768]{2,0,1:T(2,128)(2,1)}), bf16[2,1024,768]{2,0,1:T(2,128)(2,1)}, u32[]{:S(2)}, u32[]{:S(2)}) async-start(bf16[2,1024,768]{2,0,1:T(2,128)(2,1)} %copy.86), calls=%async_computation.1 | async-start | bytes 6291456 | tf_op jit(solution)/shard_map/all_to_all | solution.py:214
  437.6 193.7 %all-reduce.7.cloned.1.call-start = ((), (), s32[]{:S(2)}) async-start(), calls=%async_computation.2 | async-start | bytes 7077888 | tf_op jit(solution)/shard_map/psum | solution.py:13
  437.6 4.3 copy-start.11
  437.6 4.3 copy-start.12
  444.0 324.2 %all-reduce.11.cloned.1.call-start = ((), (), s32[]{:S(2)}) async-start(), calls=%async_computation.4 | async-start | bytes 2359296 | tf_op jit(solution)/shard_map/psum | solution.py:161
  444.1 1.9 copy-start.2
  448.4 182.9 %copy-start.4 = (bf16[2,1024,384]{2,1,0:T(8,128)(2,1)S(1)}, bf16[2,1024,384]{2,1,0:T(8,128)(2,1)}, u32[]{:S(2)}) copy-start(bf16[2,1024,384]{2,1,0:T(8,128)(2,1)} %get-tuple-element.71) | copy-start | bytes 4718596
  448.4 182.9 %copy-start.6 = (f32[384,768]{1,0:T(8,128)S(1)}, f32[384,768]{1,0:T(8,128)}, u32[]{:S(2)}) copy-start(f32[384,768]{1,0:T(8,128)} %param.21) | copy-start | bytes 3538948
  448.4 183.0 %copy-start.18 = (f32[768]{0:T(1024)S(1)}, f32[768]{0:T(1024)}, u32[]{:S(2)}) copy-start(f32[768]{0:T(1024)} %param.22) | copy-start | bytes 9220
  448.5 396.0 %all-reduce.9.cloned.1.call-start = ((), (), s32[]{:S(2)}) async-start(), calls=%async_computation.3 | async-start | bytes 7077888 | tf_op jit(solution)/shard_map/psum | solution.py:14
  844.5 4.1 copy-start.13
Sparse Core Ops, SparseCore 0:
  444.2 187.1 all-reduce.6
  638.2 130.0 all-reduce.10
  770.7 73.7 all-reduce.8
